TPU v7x, 1024 devices: a whole 8x8x8 slice. The times are simulated.
1024 devices in a mesh: row: 64 (over x, y), col: 16 (over z, core).
Axes of the slice: x: 8, y: 8, z: 8, core: 2. Of those that a mesh axis runs over, the one named last changes fastest.
Arguments:
- similarity: bfloat16 [7168, 7168], P('row', 'col'), may hold values from 0.0099487305 to 1
- in_pattern: int32 [56, 56], replicated, may hold values 0 or 1
- out_pattern: int32 [56, 56], replicated, may hold values 0 or 1
Outputs:
- inflated: bfloat16 [7168, 7168], P('row', 'col')
All inputs are finite; a program needn't handle non-finite values.
Results may differ from a plain program's by a relative error of at most 0.0029.
Values may be sent and summed in bfloat16 or wider, within the bound.
No kernel may reach another device: no remote copies, remote signals or barrier semaphores. Data moves between devices by JAX's collectives and lax.ppermute only.
A program may use at most 32 MiB of HBM per device.

v0:
```python
import jax
import jax.numpy as jnp
from jax import lax
from jax.sharding import Mesh
from jax.sharding import PartitionSpec as P


BLK = 128
F32 = jnp.float32
BF16 = jnp.bfloat16
SCALE = 32.0

def local_mask(pattern, row_start, rows, col_start, cols):
    blocks = pattern.shape[0]
    row_blocks = (row_start + lax.broadcasted_iota(jnp.int32, (rows, blocks), 0)) // BLK
    pick_row = (row_blocks == lax.broadcasted_iota(jnp.int32, (rows, blocks), 1)).astype(BF16)
    col_blocks = (col_start + lax.broadcasted_iota(jnp.int32, (blocks, cols), 1)) // BLK
    pick_col = (col_blocks == lax.broadcasted_iota(jnp.int32, (blocks, cols), 0)).astype(BF16)
    eye = jnp.eye(blocks, dtype=jnp.int32)
    kept = jnp.maximum(pattern, eye).astype(BF16)
    by_row = jnp.dot(pick_row, kept, preferred_element_type=F32).astype(BF16)
    return jnp.dot(by_row, pick_col, preferred_element_type=F32) > 0.5

def send_all(v, axes, count):
    return jnp.sum(lax.all_to_all(jnp.broadcast_to(v, (count,) + v.shape), axes, 0, 0), axis=0)

def split3(v):
    hi = v.astype(BF16)
    rest = v - hi.astype(F32)
    mid = rest.astype(BF16)
    return hi, mid, (rest - mid.astype(F32)).astype(BF16)


def body(similarity, in_pattern, out_pattern):
    rows, cols = similarity.shape
    x, quad, spot = lax.axis_index("x"), lax.axis_index("quad"), lax.axis_index("spot")
    z, core = lax.axis_index("z"), lax.axis_index("core")
    n, m = lax.axis_size("x"), lax.axis_size("spot")
    order = rows * n * n
    row_start = (x * n + quad * m + spot) * rows
    col_start = (z * 2 + core) * cols
    swap = [(0, 1), (1, 0)]
    in_mask = local_mask(in_pattern, row_start, rows, col_start, cols)
    masked = jnp.where(in_mask, similarity, jnp.zeros_like(similarity))
    own_sums = jnp.sum(masked.astype(F32), axis=0)

    mine = masked.astype(jnp.float16)
    other = lax.ppermute(mine, "quad", swap)
    part = jnp.pad(own_sums, (0, 512 - cols)).reshape(4, 128)
    part = send_all(part, ("x", "quad"), 2 * n).reshape(1, 512)[:, :cols]
    left = jnp.concatenate([masked, *split3(part), jnp.zeros((128 - rows - 3, cols), BF16)])
    left = jnp.broadcast_to(left.T.reshape(m, 1, rows, 128), (m, n, rows, 128))
    left = lax.all_to_all(left.reshape(m * n, rows, 128), ("spot", "z"), 0, 0)
    left = left.reshape(m, n, rows, 128)
    right = jnp.where(quad == 0, jnp.concatenate([mine, other]), jnp.concatenate([other, mine]))
    right = lax.all_gather(right, "x", tiled=True)
    left, right = lax.optimization_barrier((left, right))
    in_sums = jnp.sum(jnp.sum(left[..., rows : rows + 3].astype(F32), axis=0), axis=-1, keepdims=True)
    left_own = (left[..., :rows].astype(F32) / in_sums).astype(BF16)
    left_other = lax.ppermute(left_own, "core", swap)
    halves = right.reshape(n, 2, rows, cols)

    def times(l, which):
        r = lax.dynamic_index_in_dim(halves, which, 1, False).reshape(n * rows, cols).astype(BF16)
        l = l.reshape(m, n * rows, rows)
        return lax.dot_general(l, r, (((1,), (0,)), ((), ())), preferred_element_type=F32)

    partial = times(left_own, core) + times(left_other, 1 - core)
    partial = (partial * F32(SCALE)).astype(jnp.float16)
    partials = lax.all_to_all(partial, "spot", 0, 0)
    product = jnp.sum(partials.astype(F32), axis=0) * F32(1.0 / SCALE)
    out_mask = local_mask(out_pattern, row_start, rows, col_start, cols)
    product = jnp.where(out_mask, product, F32(0.0))
    sums = jnp.concatenate([jnp.sum(product * product, axis=0), own_sums, jnp.zeros((1024 - 2 * cols,), F32)])
    sums = send_all(sums.reshape(8, 128), ("x", "quad", "spot"), n * n).reshape(1024)
    own_in = sums[cols : 2 * cols]
    expanded = product / own_in
    out_sums = sums[:cols] / (own_in * own_in)
    return (F32(order) * (expanded * expanded) / out_sums).astype(BF16)

def solution(mesh):
    fine = Mesh(mesh.devices.reshape(8, 2, 4, 8, 2), ("x", "quad", "spot", "z", "core"))
    cells = P(("x", "quad", "spot"), ("z", "core"))

    return jax.shard_map(body, mesh=fine, in_specs=(cells, P(), P()), out_specs=cells, check_vma=False)
```

profile of v0, /device:TPU:16, one launch (start us, length us, event | category | flops | bytes accessed | tf_op | source)
XLA Modules:
  0.0 142.6 jit_solution(2042971496709252245)
XLA Ops:
  0.1 1.4 convert_reduce_fusion.2
  1.5 24.2 %all_to_all.20 = f32[16,4,128]{2,1,0:T(4,128)S(1)} all-to-all(f32[16,4,128]{2,1,0:T(4,128)S(1)} %broadcast_in_dim.29), channel_id=1, replica_groups=mesh['x'=8,'quad'=2,'spot'=4,'z'=8,'core'=2] {'x','quad'}, dimensions={0} | all-to-all | bytes 65536 | tf_op jit(solution)/shard_map/all_to_all | solution.py:25
  25.7 0.2 concatenate.12
  25.9 0.1 copy.18
  26.0 1.1 broadcast_in_dim.32
  27.1 18.8 %all-to-all-start.1 = ((bf16[32,112,128]{2,1,0:T(8,128)(2,1)}), bf16[32,112,128]{2,1,0:T(8,128)(2,1)S(1)}, u32[]{:S(2)}, u32[]{:S(2)}) async-start(bf16[32,112,128]{2,1,0:T(8,128)(2,1)} %bitcast.4), calls=%async_computation.1 | async-start | bytes 1835008 | tf_op jit(solution)/shard_map/all_to_all | solution.py:53
  45.9 2.5 %collective-permute-start = (f16[112,448]{1,0:T(8,128)(2,1)S(1)}, f16[112,448]{1,0:T(8,128)(2,1)S(1)}, u32[]{:S(2)}, u32[]{:S(2)}) collective-permute-start(f16[112,448]{1,0:T(8,128)(2,1)S(1)} %convert_element_type.86), channel_id=1, source_target_pairs={{0,64},{64,0},{1,65},{65,1},{2,66},{66,2},{3,67},{67,3},{4,68},{68... | collective-permute-start | bytes 301064 | tf_op jit(solution)/shard_map/ppermute | solution.py:48
  48.4 10.1 %collective-permute-done = f16[112,448]{1,0:T(8,128)(2,1)S(1)} collective-permute-done((f16[112,448]{1,0:T(8,128)(2,1)S(1)}, f16[112,448]{1,0:T(8,128)(2,1)S(1)}, u32[]{:S(2)}, u32[]{:S(2)}) %collective-permute-start) | collective-permute-done | bytes 100384 | tf_op jit(solution)/shard_map/ppermute | solution.py:48
  58.5 0.1 maximum_select_fusion
  58.6 29.3 %all-gather.1 = f16[1792,448]{1,0:T(8,128)(2,1)S(1)} all-gather(f16[224,448]{1,0:T(8,128)(2,1)S(1)} %maximum_select_fusion), channel_id=1, replica_groups=mesh['x'=8,'quad'=2,'spot'=4,'z'=8,'core'=2] {'x'}, dimensions={0}, use_global_device_ids=true | all-gather | bytes 1806336 | tf_op jit(solution)/shard_map/all_gather | solution.py:56
  87.9 0.0 all-to-all-done.1
  87.9 0.5 convert_reduce_fusion
  88.4 1.2 divide_convert_fusion
  89.7 1.9 %collective-permute-start.1 = (bf16[4,8,112,112]{3,2,1,0:T(8,128)(2,1)}, bf16[4,8,112,112]{3,2,1,0:T(8,128)(2,1)S(1)}, u32[]{:S(2)}, u32[]{:S(2)}) collective-permute-start(bf16[4,8,112,112]{3,2,1,0:T(8,128)(2,1)} %divide_convert_fusion), channel_id=1, source_target_pairs={{0,1},{1,0},{2,3},{3,2},{4,5},{5,4},{6,7},{7,6},{8,9},{9,8},{10,11... | collective-permute-start | bytes 2408456 | tf_op jit(solution)/shard_map/ppermute | solution.py:60
  91.6 0.3 dynamic-slice_convert_fusion
  91.9 1.8 %fusion.37 = f32[4,112,448]{2,1,0:T(8,128)S(1)} fusion(bf16[4,896,112]{2,1,0:T(8,128)(2,1)} %bitcast.6, bf16[896,448,1]{1,0,2:T(8,128)(2,1)S(1)} %bitcast.29), kind=kOutput, calls=%fused_computation.60 | convolution fusion | flops 359661568 | bytes 2408448 | tf_op jit(solution)/shard_map/dot_general | solution.py:66
  93.8 0.4 collective-permute-done.1
  94.2 0.0 copy-start
  94.2 0.7 fusion.1
  94.9 22.3 %all_to_all.21 = f16[4,112,448]{2,1,0:T(8,128)(2,1)S(1)} all-to-all(f16[4,112,448]{2,1,0:T(8,128)(2,1)S(1)} %fusion.1), channel_id=1, replica_groups=mesh['x'=8,'quad'=2,'spot'=4,'z'=8,'core'=2] {'spot'}, dimensions={0} | all-to-all | bytes 802816 | tf_op jit(solution)/shard_map/all_to_all | solution.py:70
  117.2 0.1 convert_reduce_fusion.1
  117.3 0.0 copy-done
  117.3 0.5 multiply_reduce_fusion
  117.8 0.1 maximum_bitcast_fusion
  117.9 23.9 %all_to_all.22 = f32[64,8,128]{2,1,0:T(8,128)S(1)} all-to-all(f32[64,8,128]{2,1,0:T(8,128)S(1)} %broadcast_in_dim.35), channel_id=1, replica_groups=mesh['x'=8,'quad'=2,'spot'=4,'z'=8,'core'=2] {'x','quad','spot'}, dimensions={0} | all-to-all | bytes 524288 | tf_op jit(solution)/shard_map/all_to_all | solution.py:25
  141.8 0.1 reduce_sum.63
  141.8 0.1 fusion.32
  141.9 0.7 divide_convert_fusion.1
  (13 shorter events, 0.1 us)
Async XLA Ops:
  27.1 60.8 %all-to-all-start.1 = ((bf16[32,112,128]{2,1,0:T(8,128)(2,1)}), bf16[32,112,128]{2,1,0:T(8,128)(2,1)S(1)}, u32[]{:S(2)}, u32[]{:S(2)}) async-start(bf16[32,112,128]{2,1,0:T(8,128)(2,1)} %bitcast.4), calls=%async_computation.1 | async-start | bytes 1835008 | tf_op jit(solution)/shard_map/all_to_all | solution.py:53
  45.9 12.6 %collective-permute-start = (f16[112,448]{1,0:T(8,128)(2,1)S(1)}, f16[112,448]{1,0:T(8,128)(2,1)S(1)}, u32[]{:S(2)}, u32[]{:S(2)}) collective-permute-start(f16[112,448]{1,0:T(8,128)(2,1)S(1)} %convert_element_type.86), channel_id=1, source_target_pairs={{0,64},{64,0},{1,65},{65,1},{2,66},{66,2},{3,67},{67,3},{4,68},{68... | collective-permute-start | bytes 301064 | tf_op jit(solution)/shard_map/ppermute | solution.py:48
  89.7 4.6 %collective-permute-start.1 = (bf16[4,8,112,112]{3,2,1,0:T(8,128)(2,1)}, bf16[4,8,112,112]{3,2,1,0:T(8,128)(2,1)S(1)}, u32[]{:S(2)}, u32[]{:S(2)}) collective-permute-start(bf16[4,8,112,112]{3,2,1,0:T(8,128)(2,1)} %divide_convert_fusion), channel_id=1, source_target_pairs={{0,1},{1,0},{2,3},{3,2},{4,5},{5,4},{6,7},{7,6},{8,9},{9,8},{10,11... | collective-permute-start | bytes 2408456 | tf_op jit(solution)/shard_map/ppermute | solution.py:60
  94.2 23.0 %copy-start = (s32[56,56]{1,0:T(8,128)S(1)}, s32[56,56]{1,0:T(8,128)}, u32[]{:S(2)}) copy-start(s32[56,56]{1,0:T(8,128)} %param.5) | copy-start | bytes 37636
where the time goes:
time: 143 us
  blocking collectives  99.7 us (70%)
  starting transfers between devices  23.2 us (16%)
  waiting for transfers between devices  10.5 us (7%)
  matrix products  4.43 us (3%)
  other arithmetic  3.28 us (2%)
    all_to_all x2, blocking collectives, send_all(): lax.all_to_all(jnp.broadcast_to(v, (count,) + v.shape), axes, 0, 0)  48.1 us
    all_gather x1, blocking collectives, body(): right = lax.all_gather(right, 'x', tiled=True)  29.3 us
    all_to_all x1, blocking collectives, body(): partials = lax.all_to_all(partial, 'spot', 0, 0)  22.3 us
    all_to_all x1, starting transfers between devices, body(): left = lax.all_to_all(left.reshape(m * n, rows, 128), ('spot', 'z'), 0, 0)  18.8 us
    ppermute x1, waiting for transfers between devices, body(): other = lax.ppermute(mine, 'quad', swap)  10.1 us
  transfers between devices with their start and end apart: 3, of which 2 were waited for; matrix products, arithmetic and copies ran while one was open for 2% of the time, Pallas kernels for 0%

commit v1 on v0

--- a/solution.py
+++ b/solution.py
@@ -55,17 +55,17 @@
     right = jnp.where(quad == 0, jnp.concatenate([mine, other]), jnp.concatenate([other, mine]))
     right = lax.all_gather(right, "x", tiled=True)
     left, right = lax.optimization_barrier((left, right))
-    in_sums = jnp.sum(jnp.sum(left[..., rows : rows + 3].astype(F32), axis=0), axis=-1, keepdims=True)
-    left_own = (left[..., :rows].astype(F32) / in_sums).astype(BF16)
-    left_other = lax.ppermute(left_own, "core", swap)
+    other = lax.ppermute(left, "core", swap)
     halves = right.reshape(n, 2, rows, cols)
 
     def times(l, which):
-        r = lax.dynamic_index_in_dim(halves, which, 1, False).reshape(n * rows, cols).astype(BF16)
-        l = l.reshape(m, n * rows, rows)
+        in_sums = jnp.sum(jnp.sum(l[..., rows : rows + 3].astype(F32), axis=0), axis=-1, keepdims=True)
+        r = lax.dynamic_index_in_dim(halves, which, 1, False).astype(F32) / in_sums
+        r = r.astype(BF16).reshape(n * rows, cols)
+        l = l.reshape(m, n * rows, 128)
         return lax.dot_general(l, r, (((1,), (0,)), ((), ())), preferred_element_type=F32)
 
-    partial = times(left_own, core) + times(left_other, 1 - core)
+    partial = (times(left, core) + times(other, 1 - core))[:, :rows]
     partial = (partial * F32(SCALE)).astype(jnp.float16)
     partials = lax.all_to_all(partial, "spot", 0, 0)
     product = jnp.sum(partials.astype(F32), axis=0) * F32(1.0 / SCALE)

time: 143 us -> 145 us (1.014)
    reduce_sum x1 -> x2, other arithmetic: 0.52 us -> 2.22 us  [times(): jnp.sum(jnp.sum(l[..., rows:rows + 3].astype(F32), axis=0), axis=-1, keep...]
  transfers between devices with their start and end apart: 3 -> 3, of which waited for: 2 -> 2; matrix products, arithmetic and copies ran while one was open for 2% -> 1% of each run, Pallas kernels for 0% -> 0%
where the time goes in v1:
time: 145 us; the launch traced here: 144 us
  blocking collectives  99.7 us (69%)
  starting transfers between devices  23.2 us (16%)
  waiting for transfers between devices  11.3 us (8%)
  matrix products  4.71 us (3%)
  other arithmetic  3.62 us (2%)
    all_to_all x2, blocking collectives, send_all(): lax.all_to_all(jnp.broadcast_to(v, (count,) + v.shape), axes, 0, 0)  48.1 us
    all_gather x1, blocking collectives, body(): right = lax.all_gather(right, 'x', tiled=True)  29.3 us
    all_to_all x1, blocking collectives, body(): partials = lax.all_to_all(partial, 'spot', 0, 0)  22.3 us
    all_to_all x1, starting transfers between devices, body(): left = lax.all_to_all(left.reshape(m * n, rows, 128), ('spot', 'z'), 0, 0)  18.8 us
    ppermute x1, waiting for transfers between devices, body(): other = lax.ppermute(mine, 'quad', swap)  10.1 us
  transfers between devices with their start and end apart: 3, of which 2 were waited for; matrix products, arithmetic and copies ran while one was open for 1% of the time, Pallas kernels for 0%

profile of v1, /device:TPU:16, one launch (start us, length us, event | category | flops | bytes accessed | tf_op | source)
XLA Modules:
  0.0 144.0 jit_solution(12345417210012776994)
XLA Ops:
  0.1 1.4 convert_reduce_fusion.3
  1.5 24.2 %all_to_all.20 = f32[16,4,128]{2,1,0:T(4,128)S(1)} all-to-all(f32[16,4,128]{2,1,0:T(4,128)S(1)} %broadcast_in_dim.31), channel_id=1, replica_groups=mesh['x'=8,'quad'=2,'spot'=4,'z'=8,'core'=2] {'x','quad'}, dimensions={0} | all-to-all | bytes 65536 | tf_op jit(solution)/shard_map/all_to_all | solution.py:25
  25.7 0.2 concatenate.12
  25.9 0.1 copy.14
  26.0 1.1 broadcast_in_dim.34
  27.1 18.8 %all-to-all-start.1 = ((bf16[32,112,128]{2,1,0:T(8,128)(2,1)}), bf16[32,112,128]{2,1,0:T(8,128)(2,1)S(1)}, u32[]{:S(2)}, u32[]{:S(2)}) async-start(bf16[32,112,128]{2,1,0:T(8,128)(2,1)} %bitcast.4), calls=%async_computation.1 | async-start | bytes 1835008 | tf_op jit(solution)/shard_map/all_to_all | solution.py:53
  45.9 2.5 %collective-permute-start = (f16[112,448]{1,0:T(8,128)(2,1)S(1)}, f16[112,448]{1,0:T(8,128)(2,1)S(1)}, u32[]{:S(2)}, u32[]{:S(2)}) collective-permute-start(f16[112,448]{1,0:T(8,128)(2,1)S(1)} %convert_element_type.89), channel_id=1, source_target_pairs={{0,64},{64,0},{1,65},{65,1},{2,66},{66,2},{3,67},{67,3},{4,68},{68... | collective-permute-start | bytes 301064 | tf_op jit(solution)/shard_map/ppermute | solution.py:48
  48.4 10.1 %collective-permute-done = f16[112,448]{1,0:T(8,128)(2,1)S(1)} collective-permute-done((f16[112,448]{1,0:T(8,128)(2,1)S(1)}, f16[112,448]{1,0:T(8,128)(2,1)S(1)}, u32[]{:S(2)}, u32[]{:S(2)}) %collective-permute-start) | collective-permute-done | bytes 100384 | tf_op jit(solution)/shard_map/ppermute | solution.py:48
  58.5 0.1 maximum_select_fusion
  58.6 29.3 %all-gather.1 = f16[1792,448]{1,0:T(8,128)(2,1)S(1)} all-gather(f16[224,448]{1,0:T(8,128)(2,1)S(1)} %maximum_select_fusion), channel_id=1, replica_groups=mesh['x'=8,'quad'=2,'spot'=4,'z'=8,'core'=2] {'x'}, dimensions={0}, use_global_device_ids=true | all-gather | bytes 1806336 | tf_op jit(solution)/shard_map/all_gather | solution.py:56
  87.9 0.0 all-to-all-done.1
  87.9 1.9 %collective-permute-start.1 = (bf16[4,8,112,128]{3,2,1,0:T(8,128)(2,1)S(1)}, bf16[4,8,112,128]{3,2,1,0:T(8,128)(2,1)}, u32[]{:S(2)}, u32[]{:S(2)}) collective-permute-start(bf16[4,8,112,128]{3,2,1,0:T(8,128)(2,1)S(1)} %bitcast.41), channel_id=1, source_target_pairs={{0,1},{1,0},{2,3},{3,2},{4,5},{5,4},{6,7},{7,6},{8,9},{9,8},{10,11... | collective-permute-start | bytes 2752520 | tf_op jit(solution)/shard_map/ppermute | solution.py:58
  89.8 0.5 convert_reduce_fusion.1
  90.4 0.8 convolution_bitcast_fusion.1
  91.2 1.2 collective-permute-done.1
  92.4 1.7 %convert_reduce_fusion = f32[8,112]{1,0:T(8,128)S(1)} fusion(bf16[4,8,112,128]{3,2,1,0:T(8,128)(2,1)} %collective-permute-done.1), kind=kLoop, calls=%fused_computation.4 | loop fusion | flops 20608 | bytes 25088 | tf_op jit(solution)/shard_map/reduce_sum | solution.py:62
  94.1 2.0 %convolution_bitcast_fusion = f32[4,128,448]{2,1,0:T(8,128)S(1)} fusion(bf16[4,8,112,128]{3,2,1,0:T(8,128)(2,1)} %collective-permute-done.1, f32[8,112]{1,0:T(8,128)S(1)} %convert_reduce_fusion, f16[8,2,112,448]{3,2,1,0:T(8,128)(2,1)S(1)} %bitcast.45, s32[]{:T(128)S(6)} %select_n.41), kind=kOutput, calls=%fused_computation.6 | convolution fusion | flops 412246016 | bytes 2756612 | tf_op jit(solution)/shard_map/dot_general | solution.py:66
  96.1 0.0 copy-start
  96.1 0.2 fusion.9
  96.4 22.3 %all_to_all.21 = f16[4,112,448]{2,1,0:T(8,128)(2,1)S(1)} all-to-all(f16[4,112,448]{2,1,0:T(8,128)(2,1)S(1)} %fusion.9), channel_id=1, replica_groups=mesh['x'=8,'quad'=2,'spot'=4,'z'=8,'core'=2] {'spot'}, dimensions={0} | all-to-all | bytes 802816 | tf_op jit(solution)/shard_map/all_to_all | solution.py:70
  118.6 0.1 convert_reduce_fusion.2
  118.7 0.0 copy-done
  118.7 0.5 multiply_reduce_fusion
  119.2 0.1 maximum_bitcast_fusion
  119.3 23.9 %all_to_all.22 = f32[64,8,128]{2,1,0:T(8,128)S(1)} all-to-all(f32[64,8,128]{2,1,0:T(8,128)S(1)} %broadcast_in_dim.37), channel_id=1, replica_groups=mesh['x'=8,'quad'=2,'spot'=4,'z'=8,'core'=2] {'x','quad','spot'}, dimensions={0} | all-to-all | bytes 524288 | tf_op jit(solution)/shard_map/all_to_all | solution.py:25
  143.2 0.1 reduce_sum.77
  143.3 0.1 fusion.46
  143.3 0.7 divide_convert_fusion
  (13 shorter events, 0.1 us)
Async XLA Ops:
  27.1 60.8 %all-to-all-start.1 = ((bf16[32,112,128]{2,1,0:T(8,128)(2,1)}), bf16[32,112,128]{2,1,0:T(8,128)(2,1)S(1)}, u32[]{:S(2)}, u32[]{:S(2)}) async-start(bf16[32,112,128]{2,1,0:T(8,128)(2,1)} %bitcast.4), calls=%async_computation.1 | async-start | bytes 1835008 | tf_op jit(solution)/shard_map/all_to_all | solution.py:53
  45.9 12.6 %collective-permute-start = (f16[112,448]{1,0:T(8,128)(2,1)S(1)}, f16[112,448]{1,0:T(8,128)(2,1)S(1)}, u32[]{:S(2)}, u32[]{:S(2)}) collective-permute-start(f16[112,448]{1,0:T(8,128)(2,1)S(1)} %convert_element_type.89), channel_id=1, source_target_pairs={{0,64},{64,0},{1,65},{65,1},{2,66},{66,2},{3,67},{67,3},{4,68},{68... | collective-permute-start | bytes 301064 | tf_op jit(solution)/shard_map/ppermute | solution.py:48
  87.9 4.5 %collective-permute-start.1 = (bf16[4,8,112,128]{3,2,1,0:T(8,128)(2,1)S(1)}, bf16[4,8,112,128]{3,2,1,0:T(8,128)(2,1)}, u32[]{:S(2)}, u32[]{:S(2)}) collective-permute-start(bf16[4,8,112,128]{3,2,1,0:T(8,128)(2,1)S(1)} %bitcast.41), channel_id=1, source_target_pairs={{0,1},{1,0},{2,3},{3,2},{4,5},{5,4},{6,7},{7,6},{8,9},{9,8},{10,11... | collective-permute-start | bytes 2752520 | tf_op jit(solution)/shard_map/ppermute | solution.py:58
  96.1 22.6 %copy-start = (s32[56,56]{1,0:T(8,128)S(1)}, s32[56,56]{1,0:T(8,128)}, u32[]{:S(2)}) copy-start(s32[56,56]{1,0:T(8,128)} %param.5) | copy-start | bytes 37636
